TPU v7x, 32 devices: a whole 2x2x4 slice. The times are simulated.
32 devices in a mesh: group: 4 (over z), member: 8 (over y, x, core).
Axes of the slice: x: 2, y: 2, z: 4, core: 2. Of those that a mesh axis runs over, the one named last changes fastest.
Arguments:
- embeddings: bfloat16 [24576, 1024], P(('group', 'member')), may hold values from -18 to 18
- prior: float32 [24576, 1000], P(('group', 'member')), may hold values from 0.05 to 5
- source_member: int32 [4, 8, 4], P('group'), may hold values from 0 to 7, as said below
- source_block: int32 [4, 8, 4], P('group'), may hold values from 0 to 5
- cross_block: int32 [4, 8, 2], P(None, 'member'), may hold values from 0 to 5
- row_links: int32 [24576, 4], P(('group', 'member')), may hold values from 0 to 5
Outputs:
- propagated: float32 [24576, 1000], P(('group', 'member'))
Inputs may be any that keep to these rules, and one draw needn't show every extreme that they name: `source_member`: no device names itself, and the members in one device's list are distinct. Over all lists of one group no member is named more than 7 times, and in every group some member is named exactly 7 times.
All inputs are finite; a program needn't handle non-finite values.
Results may differ from a plain program's by a relative error of at most 0.0079.
Values may be sent and summed in bfloat16 or wider, within the bound.
A program may use at most 64 MiB of HBM per device.

v0:
```python
import jax
import jax.numpy as jnp
from jax import lax
from jax.sharding import PartitionSpec as P

BR = 128
SERVE_CAP = 7
ITERS = 2


MIXING = 0.8


def extended(value, sides, width):
    for axis, dim in sides:
        size, length = (lax.axis_size(axis), value.shape[dim])
        up = [(i, (i + 1) % size) for i in range(size)]
        down = [(j, i) for i, j in up]
        last = lax.slice_in_dim(value, length - width, length, axis=dim)
        first = lax.slice_in_dim(value, 0, width, axis=dim)
        before = lax.ppermute(last, axis, up)
        after = lax.ppermute(first, axis, down)
        value = jnp.concatenate([before, value, after], axis=dim)
    return value


def allowed_mask(row_links, near_total, slot_total, row_count, block_rows):
    slot_ids = jnp.arange(slot_total, dtype=jnp.int32)
    slot_hits = jnp.any(row_links[:, :, None] == slot_ids[None, None, :], axis=1)
    near_mask = jnp.tile(slot_hits[:, :near_total], (1, block_rows))
    far_mask = jnp.repeat(slot_hits[:, near_total:], block_rows, axis=1)
    row_ids = lax.broadcasted_iota(jnp.int32, (row_count, row_count), 0)
    col_ids = lax.broadcasted_iota(jnp.int32, (row_count, row_count), 1)
    local_mask = row_ids != col_ids
    return jnp.concatenate([local_mask, near_mask, far_mask], axis=1)


def kernel_weights(queries, key_rows, allowed):
    features = queries.shape[1]
    scores = lax.dot_general(
        queries, key_rows, (((1,), (1,)), ((), ())), preferred_element_type=jnp.float32
    )
    scores = scores * features ** (-0.5)
    scores = jnp.where(allowed, scores, -jnp.inf)
    highest = jnp.max(scores, axis=1, keepdims=True)
    powers = jnp.where(allowed, jnp.exp(scores - highest), 0.0)
    return (powers / jnp.sum(powers, axis=1, keepdims=True)).astype(jnp.bfloat16)


def sharpen(weights, key_labels, prior_share):
    mixed = (
        MIXING * jnp.dot(weights, key_labels, preferred_element_type=jnp.float32)
        + (1.0 - MIXING) * prior_share
    )
    squared = mixed * mixed
    return squared / jnp.sum(squared, axis=1, keepdims=True)


def near_keys(delivered):
    return delivered.reshape(-1, delivered.shape[-1])


def far_keys(padded):
    return jnp.concatenate([padded[0], padded[-1]], axis=0)


def body(embeddings, prior, source_member, source_block, cross_block, row_links):
    member_count = lax.axis_size("member")
    group_count = lax.axis_size("group")
    group_index = lax.axis_index("group")
    member_index = lax.axis_index("member")
    row_count, features = embeddings.shape
    classes = prior.shape[1]
    block_rows = BR
    block_count = row_count // block_rows
    piece_rows = block_rows // member_count
    owners = source_member[0]
    slot_count = owners.shape[1]
    flat_owner = owners.reshape(-1)
    flat_block = source_block[0].reshape(-1)
    order_ids = jnp.arange(flat_owner.shape[0], dtype=jnp.int32)
    earlier = (flat_owner[:, None] == flat_owner[None, :]) & (
        order_ids[None, :] < order_ids[:, None]
    )
    rank_ids = jnp.sum(earlier.astype(jnp.int32), axis=1)
    serve_ids = jnp.arange(SERVE_CAP, dtype=jnp.int32)
    serving = (flat_owner[None, :] == member_index) & (rank_ids[None, :] == serve_ids[:, None])
    served_blocks = jnp.sum(jnp.where(serving, flat_block[None, :], 0), axis=1)
    relay_member = lax.broadcasted_iota(jnp.int32, (member_count, piece_rows, SERVE_CAP), 0)
    relay_row = lax.broadcasted_iota(jnp.int32, (member_count, piece_rows, SERVE_CAP), 1)
    relay_rows = (
        served_blocks[None, None, :] * block_rows + relay_member * piece_rows + relay_row
    ).reshape(-1)
    owner_grid = owners.reshape(member_count, 1, slot_count)
    rank_grid = rank_ids.reshape(member_count, 1, slot_count)
    piece_grid = lax.broadcasted_iota(jnp.int32, (member_count, piece_rows, slot_count), 1)
    deliver_rows = (
        owner_grid * (piece_rows * SERVE_CAP) + piece_grid * SERVE_CAP + rank_grid
    ).reshape(-1)
    below_group = (group_index + group_count - 1) % group_count
    above_group = (group_index + 1) % group_count
    cross_pick = jnp.stack([cross_block[below_group, 0, 1], cross_block[above_group, 0, 0]])
    allowed = allowed_mask(
        row_links, slot_count, slot_count + cross_block.shape[2], row_count, block_rows
    )
    prior_share = prior / jnp.sum(prior, axis=1, keepdims=True)
    labels = prior_share.astype(jnp.bfloat16)
    emb_blocks = embeddings.reshape(block_count, block_rows, features)

    def relay_pieces(flat_rows):
        return jnp.take(flat_rows, relay_rows, axis=0).reshape(
            member_count, piece_rows, SERVE_CAP, flat_rows.shape[-1]
        )

    def deliver_pieces(received):
        lane_count = received.shape[-1]
        picked = jnp.take(received.reshape(-1, lane_count), deliver_rows, axis=0)
        return picked.reshape(member_count, piece_rows, slot_count, lane_count)

    result = prior_share
    emb_relay = lax.all_to_all(
        relay_pieces(embeddings), "member", split_axis=0, concat_axis=0, tiled=True
    )
    emb_near = lax.all_to_all(
        deliver_pieces(emb_relay), "member", split_axis=0, concat_axis=0, tiled=True
    )
    emb_far = extended(emb_blocks[cross_pick], (("group", 0),), 1)
    key_rows = jnp.concatenate([embeddings, near_keys(emb_near), far_keys(emb_far)], axis=0)
    weights = kernel_weights(embeddings, key_rows, allowed)
    for iteration in range(ITERS):
        lab_blocks = labels.reshape(block_count, block_rows, classes)
        lab_relay = lax.all_to_all(
            relay_pieces(labels), "member", split_axis=0, concat_axis=0, tiled=True
        )
        lab_near = lax.all_to_all(
            deliver_pieces(lab_relay), "member", split_axis=0, concat_axis=0, tiled=True
        )
        lab_far = extended(lab_blocks[cross_pick], (("group", 0),), 1)
        key_labels = jnp.concatenate([labels, near_keys(lab_near), far_keys(lab_far)], axis=0)
        result = sharpen(weights, key_labels, prior_share)
        labels = result.astype(jnp.bfloat16)
    return result * classes


def solution(mesh):
    placed = (
        P(("group", "member"), None),
        P(("group", "member"), None),
        P("group", None, None),
        P("group", None, None),
        P(None, "member", None),
        P(("group", "member"), None),
    )
    return jax.shard_map(
        body, mesh=mesh, in_specs=placed, out_specs=P(("group", "member"), None), check_vma=False
    )
```

profile of v0, /device:TPU:0, one launch (start us, length us, event | category | flops | bytes accessed | tf_op | source)
XLA Modules:
  0.0 237.5 jit_solution(360324614991799356)
XLA Ops:
  0.0 0.9 copy.47
  2.5 2.1 reduce_sum.57
  4.6 1.4 fusion.38
  6.0 1.7 copy.50
  7.7 4.2 %gather_fusion.5 = bf16[896,1000]{1,0:T(8,128)(2,1)} fusion(bf16[768,1000]{1,0:T(8,128)(2,1)S(1)} %copy.50, s32[1024]{0:T(1024)S(1)} %pad_clamp_fusion.1), kind=kCustom, calls=%fused_computation.clone | custom fusion | bytes 3587584 | tf_op jit(solution)/shard_map/jit(_take)/gather | solution.py:111
  11.9 3.0 %broadcast_select_fusion.2 = bf16[896,1000]{1,0:T(8,128)(2,1)} fusion(bf16[896,1000]{1,0:T(8,128)(2,1)} %gather_fusion.5, pred[896]{0:T(1024)(128)(4,1)S(1)} %compare_and_fusion.2), kind=kLoop, calls=%fused_computation.46 | loop fusion | flops 896000 | bytes 3584896 | tf_op jit(solution)/shard_map/jit(_take)/select_n | solution.py:111
  14.9 4.0 %reshape.297 = bf16[8,16,7,1000]{3,2,1,0:T(8,128)(2,1)} reshape(bf16[896,1000]{1,0:T(8,128)(2,1)} %broadcast_select_fusion.2) | data formatting | bytes 3584000 | tf_op jit(solution)/shard_map/reshape | solution.py:111
  18.9 4.1 %copy.51 = bf16[8,16,7,1000]{3,1,2,0:T(8,128)(2,1)} copy(bf16[8,16,7,1000]{3,2,1,0:T(8,128)(2,1)} %reshape.297) | data formatting | bytes 3584000 | tf_op jit(solution)/shard_map/reshape | solution.py:111
  23.1 5.2 %all-to-all-start.2 = ((bf16[8,16,7,1000]{3,1,2,0:T(8,128)(2,1)}), bf16[8,16,7,1000]{3,1,2,0:T(8,128)(2,1)}, u32[]{:S(2)}, u32[]{:S(2)}) async-start(bf16[8,16,7,1000]{3,1,2,0:T(8,128)(2,1)} %copy.51), calls=%async_computation.2 | async-start | bytes 3670016 | tf_op jit(solution)/shard_map/all_to_all | solution.py:132
  28.5 4.2 %gather_fusion = bf16[896,1024]{1,0:T(8,128)(2,1)} fusion(bf16[768,1024]{1,0:T(8,128)(2,1)S(1)} %copy-done, s32[1024]{0:T(1024)S(1)} %pad_clamp_fusion.4), kind=kCustom, calls=%fused_computation.4 | custom fusion | bytes 3673600 | tf_op jit(solution)/shard_map/jit(_take)/gather | solution.py:111
  32.7 3.8 %gather.28 = bf16[8,16,7,1024]{3,2,1,0:T(8,128)(2,1)} reshape(bf16[896,1024]{1,0:T(8,128)(2,1)} %gather_fusion) | data formatting | bytes 3670016 | tf_op jit(solution)/shard_map/jit(_take)/gather | solution.py:111
  36.7 1.9 broadcast_select_fusion
  38.5 2.4 %copy.48 = bf16[8,16,7,1024]{3,1,2,0:T(8,128)(2,1)} copy(bf16[8,16,7,1024]{3,2,1,0:T(8,128)(2,1)S(1)} %broadcast_select_fusion) | data formatting | bytes 3670016 | tf_op jit(solution)/shard_map/jit(_take)/select_n | solution.py:111
  41.0 11.2 %all-to-all-done.2 = bf16[8,16,7,1000]{3,1,2,0:T(8,128)(2,1)} async-done(((bf16[8,16,7,1000]{3,1,2,0:T(8,128)(2,1)}), bf16[8,16,7,1000]{3,1,2,0:T(8,128)(2,1)}, u32[]{:S(2)}, u32[]{:S(2)}) %all-to-all-start.2) | async-done | bytes 1792032 | tf_op jit(solution)/shard_map/all_to_all | solution.py:132
  52.2 4.3 %all-to-all-start = ((bf16[8,16,7,1024]{3,1,2,0:T(8,128)(2,1)}), bf16[8,16,7,1024]{3,1,2,0:T(8,128)(2,1)}, u32[]{:S(2)}, u32[]{:S(2)}) async-start(bf16[8,16,7,1024]{3,1,2,0:T(8,128)(2,1)} %copy.48), calls=%async_computation | async-start | bytes 3670016 | tf_op jit(solution)/shard_map/all_to_all | solution.py:121
  56.9 4.0 %copy.52 = bf16[8,16,7,1000]{3,2,1,0:T(8,128)(2,1)} copy(bf16[8,16,7,1000]{3,1,2,0:T(8,128)(2,1)} %all-to-all-done.2) | data formatting | bytes 3584000 | tf_op jit(solution)/shard_map/all_to_all | solution.py:132
  60.9 4.0 %reshape.298 = bf16[896,1000]{1,0:T(8,128)(2,1)} reshape(bf16[8,16,7,1000]{3,2,1,0:T(8,128)(2,1)} %copy.52) | data formatting | bytes 3584000 | tf_op jit(solution)/shard_map/reshape | solution.py:117
  64.9 5.2 %gather_fusion.6 = bf16[512,1000]{1,0:T(8,128)(2,1)} fusion(bf16[896,1000]{1,0:T(8,128)(2,1)} %reshape.298, s32[1024]{0:T(1024)S(1)} %pad_clamp_fusion), kind=kCustom, calls=%fused_computation.1.clone | custom fusion | bytes 2050048 | tf_op jit(solution)/shard_map/jit(_take)/gather | solution.py:117
  70.2 2.4 broadcast_select_fusion.4
  72.5 2.2 reshape.299
  74.8 5.6 %all-to-all-done = bf16[8,16,7,1024]{3,1,2,0:T(8,128)(2,1)} async-done(((bf16[8,16,7,1024]{3,1,2,0:T(8,128)(2,1)}), bf16[8,16,7,1024]{3,1,2,0:T(8,128)(2,1)}, u32[]{:S(2)}, u32[]{:S(2)}) %all-to-all-start) | async-done | bytes 1835040 | tf_op jit(solution)/shard_map/all_to_all | solution.py:121
  80.3 4.4 %all-to-all-start.3 = ((bf16[8,16,4,1000]{3,2,1,0:T(4,128)(2,1)}), bf16[8,16,4,1000]{3,2,1,0:T(4,128)(2,1)}, u32[]{:S(2)}, u32[]{:S(2)}) async-start(bf16[8,16,4,1000]{3,2,1,0:T(4,128)(2,1)} %reshape.299), calls=%async_computation.3 | async-start | bytes 2097152 | tf_op jit(solution)/shard_map/all_to_all | solution.py:135
  85.7 4.0 %copy.49 = bf16[8,16,7,1024]{3,2,1,0:T(8,128)(2,1)} copy(bf16[8,16,7,1024]{3,1,2,0:T(8,128)(2,1)} %all-to-all-done) | data formatting | bytes 3670016 | tf_op jit(solution)/shard_map/all_to_all | solution.py:121
  89.7 3.9 %reshape.294 = bf16[896,1024]{1,0:T(8,128)(2,1)} reshape(bf16[8,16,7,1024]{3,2,1,0:T(8,128)(2,1)} %copy.49) | data formatting | bytes 3670016 | tf_op jit(solution)/shard_map/reshape | solution.py:117
  93.6 5.2 %gather_fusion.1 = bf16[512,1024]{1,0:T(8,128)(2,1)} fusion(bf16[896,1024]{1,0:T(8,128)(2,1)} %reshape.294, s32[1024]{0:T(1024)S(1)} %pad_clamp_fusion.3), kind=kCustom, calls=%fused_computation.5 | custom fusion | bytes 2099200 | tf_op jit(solution)/shard_map/jit(_take)/gather | solution.py:117
  98.8 2.2 gather.30
  101.0 2.8 %broadcast_select_fusion.5 = bf16[8,16,4,1024]{3,2,1,0:T(4,128)(2,1)} fusion(bf16[8,16,4,1024]{3,2,1,0:T(4,128)(2,1)} %gather.30, pred[8,16,4]{2,1,0:T(8,128)(4,1)S(1)} %compare_and_fusion.1), kind=kLoop, calls=%fused_computation.50 | loop fusion | flops 524288 | bytes 2097664 | tf_op jit(solution)/shard_map/jit(_take)/select_n | solution.py:117
  103.8 4.2 %all-to-all-start.1 = ((bf16[8,16,4,1024]{3,2,1,0:T(4,128)(2,1)}), bf16[8,16,4,1024]{3,2,1,0:T(4,128)(2,1)}, u32[]{:S(2)}, u32[]{:S(2)}) async-start(bf16[8,16,4,1024]{3,2,1,0:T(4,128)(2,1)} %broadcast_select_fusion.5), calls=%async_computation.1 | async-start | bytes 2097152 | tf_op jit(solution)/shard_map/all_to_all | solution.py:124
  108.1 1.4 fusion.34
  109.5 1.4 gather_fusion.2
  110.9 1.9 fusion.39
  112.8 2.1 collective-permute-start
  114.9 2.0 collective-permute-start.1
  117.0 1.6 copy.54
  118.6 2.0 gather_fusion.3
  121.5 3.8 %collective-permute-start.3 = (bf16[1,128,1000]{1,2,0:T(8,128)(2,1)}, bf16[1,128,1000]{1,2,0:T(8,128)(2,1)}, u32[]{:S(2)}, u32[]{:S(2)}) collective-permute-start(bf16[1,128,1000]{1,2,0:T(8,128)(2,1)} %get-tuple-element.12), channel_id=1, source_target_pairs={{8,0},{16,8},{24,16},{0,24},{9,1},{17,9},{25,17},{1,25},{10,2},{18... | collective-permute-start | bytes 768008 | tf_op jit(solution)/shard_map/ppermute | solution.py:22
  125.9 1.0 iota_compare_fusion
  126.9 1.5 reshape.300
  128.5 1.3 copy.55
  129.8 1.3 reshape.295
  131.2 7.1 %fusion = (f32[768]{0:T(1024)S(1)}, f32[1536,768]{1,0:T(8,128)S(1)}) fusion(pred[768,256]{0,1:T(32,128)(4,1)S(1)} %bitcast.39, pred[768,512]{0,1:T(32,128)(4,1)S(1)} %tile.10, pred[768,768]{0,1:T(32,128)(4,1)} %iota_compare_fusion, bf16[768,1024]{1,0:T(8,128)(2,1)S(1)} %copy-done, bf16[128,1024]{1,0:T(8,128)(2,1)} %bitcast.8, ...), kind=kOutput, calls=%fused_computation.13 | convolution fusion | flops 2434399488 | bytes 9047040 | tf_op jit(solution)/shard_map/dot_general | solution.py:40
  138.3 1.4 fusion.25
  140.2 1.7 copy-done.2
  142.6 4.1 %fusion.42 = (f32[768]{0:T(1024)S(1)}, f32[768,1000]{0,1:T(8,128)S(1)}) fusion(f32[768,1000]{0,1:T(8,128)S(1)} %copy-done.2, f32[768]{0:T(1024)S(1)} %reduce_sum.57, bf16[128,1000]{0,1:T(8,128)(2,1)} %bitcast.12, bf16[128,1000]{0,1:T(8,128)(2,1)} %bitcast.11, bf16[512,1000]{0,1:T(8,128)(2,1)S(1)} %copy-done.8, bf16[768,1000]{0,1:T(8,128)(2,1)S(1)} %copy-done.4, ...), kind=kOutput, calls=%fused_computation.93 | convolution fusion | flops 2385628416 | bytes 15126528 | tf_op jit(solution)/shard_map/dot_general | solution.py:52
  147.8 4.2 %gather_fusion.7 = bf16[896,1000]{1,0:T(8,128)(2,1)} fusion(bf16[768,1000]{1,0:T(8,128)(2,1)S(1)} %copy.56, s32[1024]{0:T(1024)S(1)} %pad_clamp_fusion.1), kind=kCustom, calls=%fused_computation.2.clone | custom fusion | bytes 3587584 | tf_op jit(solution)/shard_map/jit(_take)/gather | solution.py:111
  152.0 3.0 %broadcast_select_fusion.1 = bf16[896,1000]{1,0:T(8,128)(2,1)} fusion(bf16[896,1000]{1,0:T(8,128)(2,1)} %gather_fusion.7, pred[896]{0:T(1024)(128)(4,1)S(1)} %compare_and_fusion.2), kind=kLoop, calls=%fused_computation.45 | loop fusion | flops 896000 | bytes 3584896 | tf_op jit(solution)/shard_map/jit(_take)/select_n | solution.py:111
  155.0 4.0 %reshape.302 = bf16[8,16,7,1000]{3,2,1,0:T(8,128)(2,1)} reshape(bf16[896,1000]{1,0:T(8,128)(2,1)} %broadcast_select_fusion.1) | data formatting | bytes 3584000 | tf_op jit(solution)/shard_map/reshape | solution.py:111
  159.1 2.8 %copy.57 = bf16[8,16,7,1000]{3,1,2,0:T(8,128)(2,1)S(1)} copy(bf16[8,16,7,1000]{3,2,1,0:T(8,128)(2,1)} %reshape.302) | data formatting | bytes 3584000 | tf_op jit(solution)/shard_map/reshape | solution.py:111
  161.8 27.7 %all_to_all.30 = bf16[8,16,7,1000]{3,1,2,0:T(8,128)(2,1)S(1)} all-to-all(bf16[8,16,7,1000]{3,1,2,0:T(8,128)(2,1)S(1)} %copy.57), channel_id=1, replica_groups=mesh['group'=4,'member'=8] {'member'}, dimensions={0} | all-to-all | bytes 3584000 | tf_op jit(solution)/shard_map/all_to_all | solution.py:132
  189.5 2.4 %copy.58 = bf16[8,16,7,1000]{3,2,1,0:T(8,128)(2,1)} copy(bf16[8,16,7,1000]{3,1,2,0:T(8,128)(2,1)S(1)} %all_to_all.30) | data formatting | bytes 3584000 | tf_op jit(solution)/shard_map/all_to_all | solution.py:132
  191.9 4.0 %reshape.303 = bf16[896,1000]{1,0:T(8,128)(2,1)} reshape(bf16[8,16,7,1000]{3,2,1,0:T(8,128)(2,1)} %copy.58) | data formatting | bytes 3584000 | tf_op jit(solution)/shard_map/reshape | solution.py:117
  195.9 4.5 %gather_fusion.8 = bf16[512,1000]{1,0:T(8,128)(2,1)S(1)} fusion(bf16[896,1000]{1,0:T(8,128)(2,1)} %reshape.303, s32[1024]{0:T(1024)S(1)} %pad_clamp_fusion), kind=kCustom, calls=%fused_computation.3.clone | custom fusion | bytes 2050048 | tf_op jit(solution)/shard_map/jit(_take)/gather | solution.py:117
  200.4 1.1 broadcast_select_fusion.3
  201.5 2.3 reshape.304
  203.8 4.3 %all-to-all-start.5 = ((bf16[8,16,4,1000]{3,2,1,0:T(4,128)(2,1)}), bf16[8,16,4,1000]{3,2,1,0:T(4,128)(2,1)}, u32[]{:S(2)}, u32[]{:S(2)}) async-start(bf16[8,16,4,1000]{3,2,1,0:T(4,128)(2,1)} %reshape.304), calls=%async_computation.5 | async-start | bytes 2097152 | tf_op jit(solution)/shard_map/all_to_all | solution.py:135
  208.1 1.6 copy.60
  209.7 3.1 %gather_fusion.4 = bf16[2,128,1000]{1,2,0:T(8,128)(2,1)} fusion(bf16[6,128,1000]{1,2,0:T(8,128)(2,1)} %copy.60, s32[1024]{0:T(1024)} %copy-done.12), kind=kCustom, calls=%fused_computation.8 | custom fusion | bytes 1024008 | tf_op jit(solution)/shard_map/gather | solution.py:138
  212.8 1.9 fusion.40
  214.7 3.8 %collective-permute-start.5 = (bf16[1,128,1000]{1,2,0:T(8,128)(2,1)}, bf16[1,128,1000]{1,2,0:T(8,128)(2,1)}, u32[]{:S(2)}, u32[]{:S(2)}) collective-permute-start(bf16[1,128,1000]{1,2,0:T(8,128)(2,1)} %get-tuple-element.10), channel_id=1, source_target_pairs={{8,0},{16,8},{24,16},{0,24},{9,1},{17,9},{25,17},{1,25},{10,2},{18... | collective-permute-start | bytes 768008 | tf_op jit(solution)/shard_map/ppermute | solution.py:22
  218.5 5.0 %all-to-all-done.5 = bf16[8,16,4,1000]{3,2,1,0:T(4,128)(2,1)} async-done(((bf16[8,16,4,1000]{3,2,1,0:T(4,128)(2,1)}), bf16[8,16,4,1000]{3,2,1,0:T(4,128)(2,1)}, u32[]{:S(2)}, u32[]{:S(2)}) %all-to-all-start.5) | async-done | bytes 1024032 | tf_op jit(solution)/shard_map/all_to_all | solution.py:135
  223.5 2.3 reshape.305
  225.8 2.3 copy.61
  229.0 6.7 %fusion.43 = (f32[768]{0:T(1024)S(1)}, f32[768,1000]{0,1:T(8,128)S(1)}) fusion(f32[768,1000]{0,1:T(8,128)S(1)} %copy-done.3, f32[768]{0:T(1024)S(1)} %reduce_sum.57, bf16[128,1000]{0,1:T(8,128)(2,1)} %bitcast.15, bf16[128,1000]{0,1:T(8,128)(2,1)} %bitcast.14, bf16[512,1000]{0,1:T(8,128)(2,1)} %copy.61, bf16[768,1000]{0,1:T(8,128)(2,1)} %copy-done.5, ...), kind=kOutput, calls=%fused_computation.94 | convolution fusion | flops 2385628416 | bytes 15126528 | tf_op jit(solution)/shard_map/dot_general | solution.py:52
  235.7 1.9 divide_multiply_fusion
  (82 shorter events, 7.7 us)
Async XLA Ops:
  0.0 4.6 %copy-start.1 = (f32[768,1000]{0,1:T(8,128)S(1)}, f32[768,1000]{0,1:T(8,128)}, u32[]{:S(2)}) copy-start(f32[768,1000]{0,1:T(8,128)} %param.11) | copy-start | bytes 9216004
  18.9 9.6 %copy-start = (bf16[768,1024]{1,0:T(8,128)(2,1)S(1)}, bf16[768,1024]{1,0:T(8,128)(2,1)}, u32[]{:S(2)}) copy-start(bf16[768,1024]{1,0:T(8,128)(2,1)} %param.10) | copy-start | bytes 4718596
  23.1 29.1 %all-to-all-start.2 = ((bf16[8,16,7,1000]{3,1,2,0:T(8,128)(2,1)}), bf16[8,16,7,1000]{3,1,2,0:T(8,128)(2,1)}, u32[]{:S(2)}, u32[]{:S(2)}) async-start(bf16[8,16,7,1000]{3,1,2,0:T(8,128)(2,1)} %copy.51), calls=%async_computation.2 | async-start | bytes 3670016 | tf_op jit(solution)/shard_map/all_to_all | solution.py:132
  38.5 18.1 %copy-start.11 = (s32[1,8,4]{1,2,0:T(4,128)S(1)}, s32[1,8,4]{1,2,0:T(4,128)}, u32[]{:S(2)}) copy-start(s32[1,8,4]{1,2,0:T(4,128)} %param.12) | copy-start | bytes 388
  52.2 28.2 %all-to-all-start = ((bf16[8,16,7,1024]{3,1,2,0:T(8,128)(2,1)}), bf16[8,16,7,1024]{3,1,2,0:T(8,128)(2,1)}, u32[]{:S(2)}, u32[]{:S(2)}) async-start(bf16[8,16,7,1024]{3,1,2,0:T(8,128)(2,1)} %copy.48), calls=%async_computation | async-start | bytes 3670016 | tf_op jit(solution)/shard_map/all_to_all | solution.py:121
  56.9 13.2 %copy-start.13 = (pred[512]{0:T(512)(128)(4,1)}, pred[512]{0:T(512)(128)(4,1)S(1)}, u32[]{:S(2)}) copy-start(pred[512]{0:T(512)(128)(4,1)S(1)} %compare_and_fusion.3) | copy-start | bytes 1540
  70.2 14.8 %copy-start.15 = (s32[4,1,2]{0,2,1:T(2,128)S(1)}, s32[4,1,2]{0,2,1:T(2,128)}, u32[]{:S(2)}) copy-start(s32[4,1,2]{0,2,1:T(2,128)} %param.14) | copy-start | bytes 100
  80.3 23.5 %all-to-all-start.3 = ((bf16[8,16,4,1000]{3,2,1,0:T(4,128)(2,1)}), bf16[8,16,4,1000]{3,2,1,0:T(4,128)(2,1)}, u32[]{:S(2)}, u32[]{:S(2)}) async-start(bf16[8,16,4,1000]{3,2,1,0:T(4,128)(2,1)} %reshape.299), calls=%async_computation.3 | async-start | bytes 2097152 | tf_op jit(solution)/shard_map/all_to_all | solution.py:135
  103.8 25.9 %all-to-all-start.1 = ((bf16[8,16,4,1024]{3,2,1,0:T(4,128)(2,1)}), bf16[8,16,4,1024]{3,2,1,0:T(4,128)(2,1)}, u32[]{:S(2)}, u32[]{:S(2)}) async-start(bf16[8,16,4,1024]{3,2,1,0:T(4,128)(2,1)} %broadcast_select_fusion.5), calls=%async_computation.1 | async-start | bytes 2097152 | tf_op jit(solution)/shard_map/all_to_all | solution.py:124
  109.5 11.1 %copy-start.12 = (s32[1024]{0:T(1024)}, s32[1024]{0:T(1024)S(1)}, u32[]{:S(2)}) copy-start(s32[1024]{0:T(1024)S(1)} %pad_clamp_fusion.2) | copy-start | bytes 12292
  110.9 14.4 %copy-start.10 = (s32[768,4]{0,1:T(4,128)S(1)}, s32[768,4]{0,1:T(4,128)}, u32[]{:S(2)}) copy-start(s32[768,4]{0,1:T(4,128)} %param.15) | copy-start | bytes 36868
  112.8 18.3 %collective-permute-start = (bf16[1,128,1024]{2,1,0:T(8,128)(2,1)}, bf16[1,128,1024]{2,1,0:T(8,128)(2,1)}, u32[]{:S(2)}, u32[]{:S(2)}) collective-permute-start(bf16[1,128,1024]{2,1,0:T(8,128)(2,1)} %get-tuple-element.6), channel_id=1, source_target_pairs={{0,8},{8,16},{16,24},{24,0},{1,9},{9,17},{17,25},{25,1},{2,10},{10... | collective-permute-start | bytes 786440 | tf_op jit(solution)/shard_map/ppermute | solution.py:21
  114.9 16.2 %collective-permute-start.1 = (bf16[1,128,1024]{2,1,0:T(8,128)(2,1)}, bf16[1,128,1024]{2,1,0:T(8,128)(2,1)}, u32[]{:S(2)}, u32[]{:S(2)}) collective-permute-start(bf16[1,128,1024]{2,1,0:T(8,128)(2,1)} %get-tuple-element.8), channel_id=1, source_target_pairs={{8,0},{16,8},{24,16},{0,24},{9,1},{17,9},{25,17},{1,25},{10,2},{18... | collective-permute-start | bytes 786440 | tf_op jit(solution)/shard_map/ppermute | solution.py:22
  121.5 18.3 %collective-permute-start.2 = (bf16[1,128,1000]{1,2,0:T(8,128)(2,1)}, bf16[1,128,1000]{1,2,0:T(8,128)(2,1)}, u32[]{:S(2)}, u32[]{:S(2)}) collective-permute-start(bf16[1,128,1000]{1,2,0:T(8,128)(2,1)} %get-tuple-element.11), channel_id=1, source_target_pairs={{0,8},{8,16},{16,24},{24,0},{1,9},{9,17},{17,25},{25,1},{2,10},{10... | collective-permute-start | bytes 768008 | tf_op jit(solution)/shard_map/ppermute | solution.py:21
  121.5 18.7 %collective-permute-start.3 = (bf16[1,128,1000]{1,2,0:T(8,128)(2,1)}, bf16[1,128,1000]{1,2,0:T(8,128)(2,1)}, u32[]{:S(2)}, u32[]{:S(2)}) collective-permute-start(bf16[1,128,1000]{1,2,0:T(8,128)(2,1)} %get-tuple-element.12), channel_id=1, source_target_pairs={{8,0},{16,8},{24,16},{0,24},{9,1},{17,9},{25,17},{1,25},{10,2},{18... | collective-permute-start | bytes 768008 | tf_op jit(solution)/shard_map/ppermute | solution.py:22
  131.2 8.9 %copy-start.9 = (pred[768,2,128]{0,2,1:T(32,128)(4,1)}, pred[768,2,128]{0,2,1:T(32,128)(4,1)S(1)}, u32[]{:S(2)}) copy-start(pred[768,2,128]{0,2,1:T(32,128)(4,1)S(1)} %broadcast_in_dim.77) | copy-start | bytes 589828
  131.2 7.1 %copy-start.7 = (pred[768,768]{0,1:T(32,128)(4,1)S(1)}, pred[768,768]{0,1:T(32,128)(4,1)}, u32[]{:S(2)}) copy-start(pred[768,768]{0,1:T(32,128)(4,1)} %iota_compare_fusion) | copy-start | bytes 1769476
  138.3 8.5 %copy-start.6 = (f32[1536,768]{1,0:T(8,128)}, f32[1536,768]{1,0:T(8,128)S(1)}, u32[]{:S(2)}) copy-start(f32[1536,768]{1,0:T(8,128)S(1)} %get-tuple-element.16) | copy-start | bytes 14155780
  138.3 3.6 %copy-start.2 = (f32[768,1000]{0,1:T(8,128)S(1)}, f32[768,1000]{0,1:T(8,128)}, u32[]{:S(2)}) copy-start(f32[768,1000]{0,1:T(8,128)} %param.11) | copy-start | bytes 9216004
  138.3 4.0 %copy-start.4 = (bf16[768,1000]{0,1:T(8,128)(2,1)S(1)}, bf16[768,1000]{0,1:T(8,128)(2,1)}, u32[]{:S(2)}) copy-start(bf16[768,1000]{0,1:T(8,128)(2,1)} %fusion.38) | copy-start | bytes 4608004
  138.3 4.3 %copy-start.8 = (bf16[512,1000]{0,1:T(8,128)(2,1)S(1)}, bf16[512,1000]{0,1:T(8,128)(2,1)}, u32[]{:S(2)}) copy-start(bf16[512,1000]{0,1:T(8,128)(2,1)} %copy.55) | copy-start | bytes 3072004
  147.0 5.0 %copy-start.5 = (bf16[768,1000]{0,1:T(8,128)(2,1)}, bf16[768,1000]{0,1:T(8,128)(2,1)S(1)}, u32[]{:S(2)}) copy-start(bf16[768,1000]{0,1:T(8,128)(2,1)S(1)} %divide_convert_fusion.1) | copy-start | bytes 4608004
  195.9 4.5 %copy-start.14 = (pred[512]{0:T(512)(128)(4,1)S(1)}, pred[512]{0:T(512)(128)(4,1)}, u32[]{:S(2)}) copy-start(pred[512]{0:T(512)(128)(4,1)} %copy-done.13) | copy-start | bytes 1540
  203.8 19.7 %all-to-all-start.5 = ((bf16[8,16,4,1000]{3,2,1,0:T(4,128)(2,1)}), bf16[8,16,4,1000]{3,2,1,0:T(4,128)(2,1)}, u32[]{:S(2)}, u32[]{:S(2)}) async-start(bf16[8,16,4,1000]{3,2,1,0:T(4,128)(2,1)} %reshape.304), calls=%async_computation.5 | async-start | bytes 2097152 | tf_op jit(solution)/shard_map/all_to_all | solution.py:135
  209.7 19.2 %copy-start.3 = (f32[768,1000]{0,1:T(8,128)S(1)}, f32[768,1000]{0,1:T(8,128)}, u32[]{:S(2)}) copy-start(f32[768,1000]{0,1:T(8,128)} %param.11) | copy-start | bytes 9216004
  214.7 13.4 %collective-permute-start.4 = (bf16[1,128,1000]{1,2,0:T(8,128)(2,1)}, bf16[1,128,1000]{1,2,0:T(8,128)(2,1)}, u32[]{:S(2)}, u32[]{:S(2)}) collective-permute-start(bf16[1,128,1000]{1,2,0:T(8,128)(2,1)} %get-tuple-element.9), channel_id=1, source_target_pairs={{0,8},{8,16},{16,24},{24,0},{1,9},{9,17},{17,25},{25,1},{2,10},{10... | collective-permute-start | bytes 768008 | tf_op jit(solution)/shard_map/ppermute | solution.py:21
  214.7 14.2 %collective-permute-start.5 = (bf16[1,128,1000]{1,2,0:T(8,128)(2,1)}, bf16[1,128,1000]{1,2,0:T(8,128)(2,1)}, u32[]{:S(2)}, u32[]{:S(2)}) collective-permute-start(bf16[1,128,1000]{1,2,0:T(8,128)(2,1)} %get-tuple-element.10), channel_id=1, source_target_pairs={{8,0},{16,8},{24,16},{0,24},{9,1},{17,9},{25,17},{1,25},{10,2},{18... | collective-permute-start | bytes 768008 | tf_op jit(solution)/shard_map/ppermute | solution.py:22
where the time goes:
time: 239 us; the launch traced here: 238 us
  local copies, waits for them, and re-layouts  110 us (46%)
  starting transfers between devices  34.3 us (14%)
  blocking collectives  27.7 us (12%)
  other arithmetic  24.4 us (10%)
  waiting for transfers between devices  23 us (10%)
  matrix products  17.9 us (7%)
    all_to_all x1, blocking collectives, body(): lax.all_to_all(relay_pieces(labels), 'member', split_axis=0, concat_axis=...  27.7 us
    gather x4, local copies, waits for them, and re-layouts, deliver_pieces(): picked = jnp.take(received.reshape(-1, lane_count), deliver_rows, axis=0)  17.1 us
    gather x4, local copies, waits for them, and re-layouts, relay_pieces(): jnp.take(flat_rows, relay_rows, axis=0)  16.4 us
    reshape x4, local copies, waits for them, and re-layouts, relay_pieces(): jnp.take(flat_rows, relay_rows, axis=0)  15 us
    reshape x3, local copies, waits for them, and re-layouts, deliver_pieces(): picked = jnp.take(received.reshape(-1, lane_count), deliver_rows, axis=0)  12 us
    all_to_all x1, waiting for transfers between devices, body(): lax.all_to_all(relay_pieces(labels), 'member', split_axis=0, concat_axis=...  11.2 us
    dot_general x2, matrix products, sharpen(): jnp.dot(weights, key_labels, preferred_element_type=jnp.float32)  10.8 us
    ppermute x3, starting transfers between devices, extended(): after = lax.ppermute(first, axis, down)  9.67 us
  transfers between devices with their start and end apart: 11, of which 5 were waited for; matrix products, arithmetic and copies ran while one was open for 36% of the time, Pallas kernels for 0%

commit v1 on v0

--- a/solution.py
+++ b/solution.py
@@ -1,6 +1,10 @@
+import functools
+
 import jax
 import jax.numpy as jnp
 from jax import lax
+from jax.experimental import pallas as pl
+from jax.experimental.pallas import tpu as pltpu
 from jax.sharding import PartitionSpec as P
 
 BR = 128
@@ -64,7 +68,7 @@
     return jnp.concatenate([padded[0], padded[-1]], axis=0)
 
 
-def body(embeddings, prior, source_member, source_block, cross_block, row_links):
+def relay_body(embeddings, prior, source_member, source_block, cross_block, row_links):
     member_count = lax.axis_size("member")
     group_count = lax.axis_size("group")
     group_index = lax.axis_index("group")
@@ -142,7 +146,233 @@
     return result * classes
 
 
+MESH = pl.DeviceIdType.MESH
+
+
+def partner_of(member, mask, member_count):
+    bit = 1
+    while bit < member_count:
+        if mask & bit:
+            member = member + bit - 2 * bit * (member // bit % 2)
+        bit *= 2
+    return member
+
+
+def same(left, right):
+    gap = left - right
+    return 1 - jnp.minimum(gap * gap, 1)
+
+
+def direct_kernel(
+    member_count, group_count,
+    owners, blocks, cross, emb_hbm, prior_hbm, links_hbm, out_hbm,
+    emb, share, links, emb_send, emb_recv, lab, lab_send, lab_recv, scores, weights, mix, out,
+    load_sem, store_sem, send_sem, recv_sem,
+):
+    group = lax.axis_index("group")
+    me = lax.axis_index("member")
+    block_count, _, features = emb.shape
+    rows = block_count * BR
+    in_slots = owners.shape[0]
+    below = (group + group_count - 1) % group_count
+    above = (group + 1) % group_count
+    group_blocks = 2 if block_count % 2 == 0 else 1
+    width = group_blocks * BR
+    chunks = rows // width
+    slots = 2 + member_count - 1
+    partners = [partner_of(me, mask, member_count) for mask in range(1, member_count)]
+    targets = [(above, me), (below, me)] + [(group, p) for p in partners]
+    sending = list(range(slots - 1, 1, -1)) + [0, 1]
+
+    def lanes_of(c):
+        return pl.ds(pl.multiple_of(c * width, width), width)
+
+    emb_load = pltpu.make_async_copy(emb_hbm, emb, load_sem.at[0])
+    prior_load = pltpu.make_async_copy(prior_hbm, share, load_sem.at[1])
+    links_load = pltpu.make_async_copy(links_hbm, links, load_sem.at[2])
+    emb_load.start()
+    prior_load.start()
+    links_load.start()
+
+    barrier = pltpu.get_barrier_semaphore()
+    for target in targets:
+        pl.semaphore_signal(barrier, inc=1, device_id=target, device_id_type=MESH)
+
+    picks = [cross[0, above], cross[1, below]]
+    names = [jnp.int32(in_slots), jnp.int32(in_slots + 1)]
+    for p in partners:
+        pick = jnp.int32(0)
+        name = jnp.int32(-1)
+        for k in range(in_slots):
+            pick += same(owners[k, p], me) * blocks[k, p]
+            name += same(owners[k, me], p) * (k + 1)
+        picks.append(pick)
+        names.append(name)
+
+    def copy_of(stage, s):
+        src = emb_send.at[s] if stage == 0 else lab_send.at[stage - 1, s]
+        dst = emb_recv.at[s] if stage == 0 else lab_recv.at[stage - 1, s]
+        return pltpu.make_async_remote_copy(
+            src_ref=src, dst_ref=dst,
+            send_sem=send_sem.at[stage, s], recv_sem=recv_sem.at[stage, s],
+            device_id=targets[s], device_id_type=MESH,
+        )
+
+    emb_load.wait()
+    pl.semaphore_wait(barrier, slots)
+    for s in sending:
+        emb_send[s] = emb[picks[s]]
+        copy_of(0, s).start()
+
+    def put_labels(c, value):
+        value = value.astype(jnp.bfloat16)
+        for b in range(group_blocks):
+            lab[c * group_blocks + b] = value[:, b * BR:(b + 1) * BR]
+
+    def send_labels(stage):
+        for s in sending:
+            lab_send[stage - 1, s] = lab[picks[s]]
+            copy_of(stage, s).start()
+
+    prior_load.wait()
+
+    def first_labels(c, _):
+        lanes = lanes_of(c)
+        value = share[:, lanes]
+        value = value / jnp.sum(value, axis=0, keepdims=True)
+        put_labels(c, value)
+        share[:, lanes] = value
+        return _
+
+    lax.fori_loop(0, chunks, first_labels, 0)
+    send_labels(1)
+    links_load.wait()
+
+    def score_of(keys):
+        value = lax.dot_general(
+            keys, emb[...].reshape(rows, features), (((1,), (1,)), ((), ())), preferred_element_type=jnp.float32
+        )
+        return value * features ** (-0.5)
+
+    def own_scores(b, _):
+        span = pl.ds(pl.multiple_of(b * BR, BR), BR)
+        value = score_of(emb[b])
+        key_ids = lax.broadcasted_iota(jnp.int32, (BR, rows), 0) + b * BR
+        row_ids = lax.broadcasted_iota(jnp.int32, (BR, rows), 1)
+        scores[span, :] = jnp.where(key_ids != row_ids, value, -jnp.inf)
+        return _
+
+    lax.fori_loop(0, rows // BR, own_scores, 0)
+    for s in range(slots):
+        bias = jnp.max(jnp.where(links[...] == names[s], 0.0, -jnp.inf), axis=0, keepdims=True)
+        copy_of(0, s).wait_recv()
+        scores[rows + s * BR:rows + (s + 1) * BR, :] = score_of(emb_recv[s]) + bias
+
+    def soften(b, _):
+        lanes = pl.ds(pl.multiple_of(b * BR, BR), BR)
+        value = scores[:, lanes]
+        powers = jnp.exp(value - jnp.max(value, axis=0, keepdims=True))
+        total = jnp.sum(powers, axis=0, keepdims=True)
+        weights[:, lanes] = (powers * (1.0 / total)).astype(jnp.bfloat16)
+        return _
+
+    lax.fori_loop(0, rows // BR, soften, 0)
+
+    def own_mix(c, _):
+        lanes = lanes_of(c)
+        keys = jnp.concatenate([lab[b] for b in range(block_count)], axis=1)
+        mix[:, lanes] = jnp.dot(
+            keys, weights[:rows, lanes], preferred_element_type=jnp.float32
+        )
+        return _
+
+    def sharp_of(total, lanes):
+        mixed = MIXING * total + (1.0 - MIXING) * share[:, lanes]
+        squared = mixed * mixed
+        return squared / jnp.sum(squared, axis=0, keepdims=True)
+
+    spans = [(0, 3)] + [(s, min(s + 2, slots)) for s in range(3, slots, 2)]
+
+    for stage in (1, 2):
+        lax.fori_loop(0, chunks, own_mix, 0)
+        for first, last in spans:
+            for s in range(first, last):
+                copy_of(stage, s).wait_recv()
+
+            def arrived(c, _, first=first, last=last):
+                lanes = lanes_of(c)
+                keys = [lab_recv[stage - 1, s] for s in range(first, last)]
+                keys = jnp.concatenate(keys, axis=1) if len(keys) > 1 else keys[0]
+                total = mix[:, lanes] + jnp.dot(
+                    keys, weights[rows + first * BR:rows + last * BR, lanes],
+                    preferred_element_type=jnp.float32,
+                )
+                if last < slots:
+                    mix[:, lanes] = total
+                elif stage == 1:
+                    put_labels(c, sharp_of(total, lanes))
+                else:
+                    out[:, lanes] = sharp_of(total, lanes)
+                return _
+
+            lax.fori_loop(0, chunks, arrived, 0)
+        if stage == 1:
+            send_labels(2)
+    store = pltpu.make_async_copy(out, out_hbm, store_sem)
+    store.start()
+    for stage in range(ITERS + 1):
+        for s in range(slots):
+            copy_of(stage, s).wait_send()
+    store.wait()
+
+
+def direct_body(embeddings, prior, source_member, source_block, cross_block, row_links):
+    member_count = lax.axis_size("member")
+    group_count = lax.axis_size("group")
+    rows, features = embeddings.shape
+    classes = prior.shape[1]
+    slots = 2 + member_count - 1
+    keys = rows + slots * BR
+    any_space = pl.BlockSpec(memory_space=pl.ANY)
+    smem = pl.BlockSpec(memory_space=pltpu.SMEM)
+    bf16, f32 = jnp.bfloat16, jnp.float32
+    sharp = pl.pallas_call(
+        functools.partial(direct_kernel, member_count, group_count),
+        out_shape=jax.ShapeDtypeStruct((classes, rows), f32),
+        in_specs=[smem] * 3 + [any_space] * 3,
+        out_specs=any_space,
+        scratch_shapes=[
+            pltpu.VMEM((rows // BR, BR, features), bf16),
+            pltpu.VMEM((classes, rows), f32),
+            pltpu.VMEM((row_links.shape[1], rows), jnp.int32),
+            pltpu.VMEM((slots, BR, features), bf16),
+            pltpu.VMEM((slots, BR, features), bf16),
+            pltpu.VMEM((rows // BR, classes, BR), bf16),
+            pltpu.VMEM((ITERS, slots, classes, BR), bf16),
+            pltpu.VMEM((ITERS, slots, classes, BR), bf16),
+            pltpu.VMEM((keys, rows), f32),
+            pltpu.VMEM((keys, rows), bf16),
+            pltpu.VMEM((classes, rows), f32),
+            pltpu.VMEM((classes, rows), f32),
+            pltpu.SemaphoreType.DMA((3,)),
+            pltpu.SemaphoreType.DMA,
+            pltpu.SemaphoreType.DMA((ITERS + 1, slots)),
+            pltpu.SemaphoreType.DMA((ITERS + 1, slots)),
+        ],
+        compiler_params=pltpu.CompilerParams(
+            collective_id=0, has_side_effects=True, vmem_limit_bytes=60 * 2**20
+        ),
+    )(
+        source_member[0].T, source_block[0].T, cross_block[:, 0, :].T,
+        embeddings.reshape(rows // BR, BR, features), prior.T, row_links.T,
+    )
+    return sharp.T * classes
+
+
 def solution(mesh):
+    member_count = mesh.shape["member"]
+    direct = member_count & (member_count - 1) == 0 and member_count - 1 <= SERVE_CAP
+    body = direct_body if direct else relay_body
     placed = (
         P(("group", "member"), None),
         P(("group", "member"), None),

time: 239 us -> 88.3 us (0.37)
  local copies, waits for them, and re-layouts: 110 us -> 0 us
  Pallas kernels: 0 us -> 84.4 us
  starting transfers between devices: 34.3 us -> 0 us
  blocking collectives: 27.7 us -> 0 us
  waiting for transfers between devices: 23 us -> 0 us
  other arithmetic: 24.4 us -> 3.71 us
  matrix products: 17.9 us -> 0 us
    pallas_call x0 -> x1, Pallas kernels: none -> 84.4 us  [direct_body(): pl.pallas_call(functools.partial(direct_kernel, member_count, group_count...]
    reshape x16 -> x0, local copies, waits for them, and re-layouts: 43.5 us -> none  [the longest x4 15 us: relay_pieces(): jnp.take(flat_rows, relay_rows, axis=0)]
    gather x11 -> x0, local copies, waits for them, and re-layouts: 40 us -> none  [the longest x4 17.1 us: deliver_pieces(): picked = jnp.take(received.reshape(-1, lane_count), deliver_rows, axis=0)]
    all_to_all x1 -> x0, blocking collectives: 27.7 us -> none  [body(): lax.all_to_all(relay_pieces(labels), 'member', split_axis=0, concat_axis=...]
    all_to_all x5 -> x0, starting transfers between devices: 22.5 us -> none  [the longest x2 8.69 us: body(): lax.all_to_all(deliver_pieces(lab_relay), 'member', split_axis=0, concat_...]
    all_to_all x5 -> x0, waiting for transfers between devices: 21.8 us -> none  [the longest x1 11.2 us: body(): lax.all_to_all(relay_pieces(labels), 'member', split_axis=0, concat_axis=...]
    dot_general x3 -> x0, matrix products: 17.9 us -> none  [the longest x2 10.8 us: sharpen(): jnp.dot(weights, key_labels, preferred_element_type=jnp.float32)]
    select_n x11 -> x0, other arithmetic: 15.6 us -> none  [the longest x5 7.89 us: relay_pieces(): jnp.take(flat_rows, relay_rows, axis=0)]
  transfers between devices with their start and end apart: 11 -> 0, of which waited for: 5 -> 0; matrix products, arithmetic and copies ran while one was open for 36% -> 0% of each run, Pallas kernels for 0% -> 0%
where the time goes in v1:
time: 88.3 us; the launch traced here: 88.2 us
  Pallas kernels  84.4 us (96%)
  other arithmetic  3.71 us (4%)
    pallas_call x1, Pallas kernels, direct_body(): pl.pallas_call(functools.partial(direct_kernel, member_count, group_count...  84.4 us
    mul x1, other arithmetic, direct_body(): return sharp.T * classes  3.71 us

profile of v1, /device:TPU:0, one launch (start us, length us, event | category | flops | bytes accessed | tf_op | source)
XLA Modules:
  0.0 88.2 jit_solution(6403549352706551872)
XLA Ops:
  0.0 84.4 %shard_map.64 = f32[1000,768]{1,0:T(8,128)} custom-call(s32[4,8]{1,0:T(4,128)} %bitcast.17, s32[4,8]{1,0:T(4,128)} %bitcast.18, s32[2,4]{1,0:T(2,128)} %bitcast.19, bf16[6,128,1024]{2,1,0:T(8,128)(2,1)} %bitcast.15, f32[1000,768]{1,0:T(8,128)} %bitcast.14, s32[4,768]{1,0:T(4,128)} %bitcast.16), custom_call_target="tpu_custom_call" | custom-call | tf_op jit(solution)/shard_map/pallas_call | solution.py:339
  84.5 3.7 %multiply_bitcast_fusion = f32[768,1000]{0,1:T(8,128)} fusion(f32[1000,768]{1,0:T(8,128)} %shard_map.64), kind=kLoop, calls=%fused_computation | loop fusion | flops 768000 | bytes 6144000 | tf_op jit(solution)/shard_map/mul | solution.py:369

commit v2 on v1

--- a/solution.py
+++ b/solution.py
@@ -165,9 +165,9 @@
 
 def direct_kernel(
     member_count, group_count,
-    owners, blocks, cross, emb_hbm, prior_hbm, links_hbm, out_hbm,
-    emb, share, links, emb_send, emb_recv, lab, lab_send, lab_recv, scores, weights, mix, out,
-    load_sem, store_sem, send_sem, recv_sem,
+    owners, blocks, cross, emb_hbm, prior_hbm, links_hbm, out,
+    emb, share, links, emb_send, emb_recv, lab, lab_send, lab_recv, scores, weights, mix,
+    load_sem, send_sem, recv_sem,
 ):
     group = lax.axis_index("group")
     me = lax.axis_index("member")
@@ -182,7 +182,8 @@
     slots = 2 + member_count - 1
     partners = [partner_of(me, mask, member_count) for mask in range(1, member_count)]
     targets = [(above, me), (below, me)] + [(group, p) for p in partners]
-    sending = list(range(slots - 1, 1, -1)) + [0, 1]
+    masks = sorted(range(1, member_count), key=lambda mask: (mask == 1, (mask >> 1).bit_count(), mask & 1))
+    sending = [1 + mask for mask in masks] + [0, 1]
 
     def lanes_of(c):
         return pl.ds(pl.multiple_of(c * width, width), width)
@@ -318,12 +319,9 @@
             lax.fori_loop(0, chunks, arrived, 0)
         if stage == 1:
             send_labels(2)
-    store = pltpu.make_async_copy(out, out_hbm, store_sem)
-    store.start()
     for stage in range(ITERS + 1):
         for s in range(slots):
             copy_of(stage, s).wait_send()
-    store.wait()
 
 
 def direct_body(embeddings, prior, source_member, source_block, cross_block, row_links):
@@ -338,9 +336,9 @@
     bf16, f32 = jnp.bfloat16, jnp.float32
     sharp = pl.pallas_call(
         functools.partial(direct_kernel, member_count, group_count),
-        out_shape=jax.ShapeDtypeStruct((classes, rows), f32),
+        out_shape=pltpu.VMEM((classes, rows), f32),
         in_specs=[smem] * 3 + [any_space] * 3,
-        out_specs=any_space,
+        out_specs=pl.BlockSpec(memory_space=pltpu.VMEM),
         scratch_shapes=[
             pltpu.VMEM((rows // BR, BR, features), bf16),
             pltpu.VMEM((classes, rows), f32),
@@ -353,9 +351,7 @@
             pltpu.VMEM((keys, rows), f32),
             pltpu.VMEM((keys, rows), bf16),
             pltpu.VMEM((classes, rows), f32),
-            pltpu.VMEM((classes, rows), f32),
             pltpu.SemaphoreType.DMA((3,)),
-            pltpu.SemaphoreType.DMA,
             pltpu.SemaphoreType.DMA((ITERS + 1, slots)),
             pltpu.SemaphoreType.DMA((ITERS + 1, slots)),
         ],

time: 88.3 us -> 81.7 us (0.925)
  Pallas kernels: 84.4 us -> 79.7 us
  other arithmetic: 3.71 us -> 1.84 us
    pallas_call x1, Pallas kernels: 84.4 us -> 79.7 us  [direct_body(): pl.pallas_call(functools.partial(direct_kernel, member_count, group_count...]
    mul x1, other arithmetic: 3.71 us -> 1.84 us  [direct_body(): return sharp.T * classes]
where the time goes in v2:
time: 81.7 us; the launch traced here: 81.5 us
  Pallas kernels  79.7 us (98%)
  other arithmetic  1.84 us (2%)
    pallas_call x1, Pallas kernels, direct_body(): pl.pallas_call(functools.partial(direct_kernel, member_count, group_count...  79.7 us
    mul x1, other arithmetic, direct_body(): return sharp.T * classes  1.84 us

profile of v2, /device:TPU:0, one launch (start us, length us, event | category | flops | bytes accessed | tf_op | source)
XLA Modules:
  0.0 81.5 jit_solution(17010487885500617041)
XLA Ops:
  0.0 79.7 %shard_map.64 = f32[1000,768]{1,0:T(8,128)S(1)} custom-call(s32[4,8]{1,0:T(4,128)} %bitcast.17, s32[4,8]{1,0:T(4,128)} %bitcast.18, s32[2,4]{1,0:T(2,128)} %bitcast.19, bf16[6,128,1024]{2,1,0:T(8,128)(2,1)} %bitcast.15, f32[1000,768]{1,0:T(8,128)} %bitcast.14, s32[4,768]{1,0:T(4,128)} %bitcast.16), custom_call_target="tpu_custom_call" | custom-call | tf_op jit(solution)/shard_map/pallas_call | solution.py:337
  79.7 1.8 %multiply_bitcast_fusion = f32[768,1000]{0,1:T(8,128)} fusion(f32[1000,768]{1,0:T(8,128)S(1)} %shard_map.64), kind=kLoop, calls=%fused_computation | loop fusion | flops 768000 | bytes 6144000 | tf_op jit(solution)/shard_map/mul | solution.py:365

commit v3 on v2

--- a/solution.py
+++ b/solution.py
@@ -166,7 +166,8 @@
 def direct_kernel(
     member_count, group_count,
     owners, blocks, cross, emb_hbm, prior_hbm, links_hbm, out,
-    emb, share, links, emb_send, emb_recv, lab, lab_send, lab_recv, scores, weights, mix,
+    emb, share, links, emb_send, emb_recv, lab_low, lab_high, send_low, send_high, recv_low, recv_high,
+    sums, sum_send, sum_recv, keys_ref, scores, weights, mix,
     load_sem, send_sem, recv_sem,
 ):
     group = lax.axis_index("group")
@@ -185,6 +186,11 @@
     masks = sorted(range(1, member_count), key=lambda mask: (mask == 1, (mask >> 1).bit_count(), mask & 1))
     sending = [1 + mask for mask in masks] + [0, 1]
 
+    labs, lab_sends, lab_recvs = (lab_low, lab_high), (send_low, send_high), (recv_low, recv_high)
+    split = lab_low.shape[1]
+    heights = (split, lab_high.shape[1])
+    bands = (slice(0, split), slice(split, split + heights[1]))
+
     def lanes_of(c):
         return pl.ds(pl.multiple_of(c * width, width), width)
 
@@ -210,14 +216,22 @@
         picks.append(pick)
         names.append(name)
 
-    def copy_of(stage, s):
-        src = emb_send.at[s] if stage == 0 else lab_send.at[stage - 1, s]
-        dst = emb_recv.at[s] if stage == 0 else lab_recv.at[stage - 1, s]
+    def copy_of(kind, s):
+        sides = [(emb_send, emb_recv)]
+        for stage in range(ITERS):
+            sides += [(lab_sends[h].at[stage], lab_recvs[h].at[stage]) for h in (0, 1)]
+        sides.append((sum_send, sum_recv))
+        src, dst = sides[kind]
         return pltpu.make_async_remote_copy(
-            src_ref=src, dst_ref=dst,
-            send_sem=send_sem.at[stage, s], recv_sem=recv_sem.at[stage, s],
+            src_ref=src.at[s], dst_ref=dst.at[s],
+            send_sem=send_sem.at[kind, s], recv_sem=recv_sem.at[kind, s],
             device_id=targets[s], device_id_type=MESH,
         )
+
+    def kind_of(stage, half):
+        return 1 + 2 * stage + half
+
+    sum_kind = 1 + 2 * ITERS
 
     emb_load.wait()
     pl.semaphore_wait(barrier, slots)
@@ -225,15 +239,15 @@
         emb_send[s] = emb[picks[s]]
         copy_of(0, s).start()
 
-    def put_labels(c, value):
+    def put_labels(half, c, value):
         value = value.astype(jnp.bfloat16)
         for b in range(group_blocks):
-            lab[c * group_blocks + b] = value[:, b * BR:(b + 1) * BR]
-
-    def send_labels(stage):
+            labs[half][c * group_blocks + b] = value[:, b * BR:(b + 1) * BR]
+
+    def send_labels(stage, half):
         for s in sending:
-            lab_send[stage - 1, s] = lab[picks[s]]
-            copy_of(stage, s).start()
+            lab_sends[half][stage, s] = labs[half][picks[s]]
+            copy_of(kind_of(stage, half), s).start()
 
     prior_load.wait()
 
@@ -241,12 +255,14 @@
         lanes = lanes_of(c)
         value = share[:, lanes]
         value = value / jnp.sum(value, axis=0, keepdims=True)
-        put_labels(c, value)
         share[:, lanes] = value
+        for half in (0, 1):
+            put_labels(half, c, value[bands[half]])
         return _
 
     lax.fori_loop(0, chunks, first_labels, 0)
-    send_labels(1)
+    send_labels(0, 0)
+    send_labels(0, 1)
     links_load.wait()
 
     def score_of(keys):
@@ -281,47 +297,97 @@
 
     def own_mix(c, _):
         lanes = lanes_of(c)
-        keys = jnp.concatenate([lab[b] for b in range(block_count)], axis=1)
-        mix[:, lanes] = jnp.dot(
-            keys, weights[:rows, lanes], preferred_element_type=jnp.float32
-        )
+        for half in (0, 1):
+            keys = jnp.concatenate([labs[half][b] for b in range(block_count)], axis=1)
+            mix[bands[half], lanes] = jnp.dot(
+                keys, weights[:rows, lanes], preferred_element_type=jnp.float32
+            )
         return _
 
-    def sharp_of(total, lanes):
-        mixed = MIXING * total + (1.0 - MIXING) * share[:, lanes]
-        squared = mixed * mixed
-        return squared / jnp.sum(squared, axis=0, keepdims=True)
+    def squared_of(total, half, lanes):
+        mixed = MIXING * total + (1.0 - MIXING) * share[bands[half], lanes]
+        return mixed * mixed
 
     spans = [(0, 3)] + [(s, min(s + 2, slots)) for s in range(3, slots, 2)]
 
-    for stage in (1, 2):
-        lax.fori_loop(0, chunks, own_mix, 0)
+    def neighbour_mix(stage, half, finish):
         for first, last in spans:
             for s in range(first, last):
-                copy_of(stage, s).wait_recv()
+                copy_of(kind_of(stage, half), s).wait_recv()
+                block = lab_recvs[half][stage, s]
+                if stage > 0:
+                    if half == 0:
+                        copy_of(sum_kind, s).wait_recv()
+                    scale = 1.0 / sum_recv[s][:1]
+                    block = (block.astype(jnp.float32) * scale).astype(jnp.bfloat16)
+                keys_ref[:heights[half], (s - first) * BR:(s - first + 1) * BR] = block
 
             def arrived(c, _, first=first, last=last):
                 lanes = lanes_of(c)
-                keys = [lab_recv[stage - 1, s] for s in range(first, last)]
-                keys = jnp.concatenate(keys, axis=1) if len(keys) > 1 else keys[0]
-                total = mix[:, lanes] + jnp.dot(
-                    keys, weights[rows + first * BR:rows + last * BR, lanes],
+                total = mix[bands[half], lanes] + jnp.dot(
+                    keys_ref[:heights[half], :(last - first) * BR],
+                    weights[rows + first * BR:rows + last * BR, lanes],
                     preferred_element_type=jnp.float32,
                 )
                 if last < slots:
-                    mix[:, lanes] = total
-                elif stage == 1:
-                    put_labels(c, sharp_of(total, lanes))
+                    mix[bands[half], lanes] = total
                 else:
-                    out[:, lanes] = sharp_of(total, lanes)
+                    finish(c, lanes, squared_of(total, half, lanes))
                 return _
 
             lax.fori_loop(0, chunks, arrived, 0)
-        if stage == 1:
-            send_labels(2)
-    for stage in range(ITERS + 1):
+
+    def put_sums(half, c, squared):
+        part = jnp.sum(squared, axis=0, keepdims=True)
+        for b in range(group_blocks):
+            value = jnp.broadcast_to(part[:, b * BR:(b + 1) * BR], (8, BR))
+            at = c * group_blocks + b
+            sums[at] = value if half == 0 else sums[at] + value
+
+    def middle(half):
+        def finish(c, lanes, squared):
+            mix[bands[half], lanes] = squared
+            put_labels(half, c, squared)
+            put_sums(half, c, squared)
+
+        return finish
+
+    def own_labels(c, _):
+        lanes = lanes_of(c)
+        parts = [sums[c * group_blocks + b][:1] for b in range(group_blocks)]
+        scale = 1.0 / jnp.concatenate(parts, axis=1)
+        for half in (0, 1):
+            put_labels(half, c, mix[bands[half], lanes] * scale)
+        return _
+
+    for stage in range(ITERS - 1):
+        lax.fori_loop(0, chunks, own_mix, 0)
+        for half in (0, 1):
+            neighbour_mix(stage, half, middle(half))
+            if half == 1:
+                for s in sending:
+                    sum_send[s] = sums[picks[s]]
+                    copy_of(sum_kind, s).start()
+            send_labels(stage + 1, half)
+        lax.fori_loop(0, chunks, own_labels, 0)
+
+    def last_low(c, lanes, squared):
+        mix[bands[0], lanes] = squared
+        put_sums(0, c, squared)
+
+    def last_high(c, lanes, squared):
+        put_sums(1, c, squared)
+        parts = [sums[c * group_blocks + b][:1] for b in range(group_blocks)]
+        scale = 1.0 / jnp.concatenate(parts, axis=1)
+        out[bands[0], lanes] = mix[bands[0], lanes] * scale
+        out[bands[1], lanes] = squared * scale
+
+    lax.fori_loop(0, chunks, own_mix, 0)
+    neighbour_mix(ITERS - 1, 0, last_low)
+    neighbour_mix(ITERS - 1, 1, last_high)
+    for kind in range(sum_kind + 1):
         for s in range(slots):
-            copy_of(stage, s).wait_send()
+            copy_of(kind, s).wait_send()
 
 
 def direct_body(embeddings, prior, source_member, source_block, cross_block, row_links):
@@ -331,6 +397,7 @@
     classes = prior.shape[1]
     slots = 2 + member_count - 1
     keys = rows + slots * BR
+    split = -(-classes // 32) * 16
     any_space = pl.BlockSpec(memory_space=pl.ANY)
     smem = pl.BlockSpec(memory_space=pltpu.SMEM)
     bf16, f32 = jnp.bfloat16, jnp.float32
@@ -345,15 +412,22 @@
             pltpu.VMEM((row_links.shape[1], rows), jnp.int32),
             pltpu.VMEM((slots, BR, features), bf16),
             pltpu.VMEM((slots, BR, features), bf16),
-            pltpu.VMEM((rows // BR, classes, BR), bf16),
-            pltpu.VMEM((ITERS, slots, classes, BR), bf16),
-            pltpu.VMEM((ITERS, slots, classes, BR), bf16),
+            pltpu.VMEM((rows // BR, split, BR), bf16),
+            pltpu.VMEM((rows // BR, classes - split, BR), bf16),
+            pltpu.VMEM((ITERS, slots, split, BR), bf16),
+            pltpu.VMEM((ITERS, slots, classes - split, BR), bf16),
+            pltpu.VMEM((ITERS, slots, split, BR), bf16),
+            pltpu.VMEM((ITERS, slots, classes - split, BR), bf16),
+            pltpu.VMEM((rows // BR, 8, BR), f32),
+            pltpu.VMEM((slots, 8, BR), f32),
+            pltpu.VMEM((slots, 8, BR), f32),
+            pltpu.VMEM((split, 3 * BR), bf16),
             pltpu.VMEM((keys, rows), f32),
             pltpu.VMEM((keys, rows), bf16),
             pltpu.VMEM((classes, rows), f32),
             pltpu.SemaphoreType.DMA((3,)),
-            pltpu.SemaphoreType.DMA((ITERS + 1, slots)),
-            pltpu.SemaphoreType.DMA((ITERS + 1, slots)),
+            pltpu.SemaphoreType.DMA((2 * ITERS + 2, slots)),
+            pltpu.SemaphoreType.DMA((2 * ITERS + 2, slots)),
         ],
         compiler_params=pltpu.CompilerParams(
             collective_id=0, has_side_effects=True, vmem_limit_bytes=60 * 2**20

time: 81.7 us -> 79.2 us (0.969)
  Pallas kernels: 79.7 us -> 76.7 us
    pallas_call x1, Pallas kernels: 79.7 us -> 76.7 us  [direct_body(): pl.pallas_call(functools.partial(direct_kernel, member_count, group_count...]
where the time goes in v3:
time: 79.2 us; the launch traced here: 78.5 us
  Pallas kernels  76.7 us (97%)
  other arithmetic  1.84 us (2%)
    pallas_call x1, Pallas kernels, direct_body(): pl.pallas_call(functools.partial(direct_kernel, member_count, group_count...  76.7 us
    mul x1, other arithmetic, direct_body(): return sharp.T * classes  1.84 us

profile of v3, /device:TPU:0, one launch (start us, length us, event | category | flops | bytes accessed | tf_op | source)
XLA Modules:
  0.0 78.5 jit_solution(17047008810152112711)
XLA Ops:
  0.0 76.7 %shard_map.64 = f32[1000,768]{1,0:T(8,128)S(1)} custom-call(s32[4,8]{1,0:T(4,128)} %bitcast.17, s32[4,8]{1,0:T(4,128)} %bitcast.18, s32[2,4]{1,0:T(2,128)} %bitcast.19, bf16[6,128,1024]{2,1,0:T(8,128)(2,1)} %bitcast.15, f32[1000,768]{1,0:T(8,128)} %bitcast.14, s32[4,768]{1,0:T(4,128)} %bitcast.16), custom_call_target="tpu_custom_call" | custom-call | tf_op jit(solution)/shard_map/pallas_call | solution.py:404
  76.7 1.8 %multiply_bitcast_fusion = f32[768,1000]{0,1:T(8,128)} fusion(f32[1000,768]{1,0:T(8,128)S(1)} %shard_map.64), kind=kLoop, calls=%fused_computation | loop fusion | flops 768000 | bytes 6144000 | tf_op jit(solution)/shard_map/mul | solution.py:439

commit v4 on v3

--- a/solution.py
+++ b/solution.py
@@ -184,7 +184,7 @@
     partners = [partner_of(me, mask, member_count) for mask in range(1, member_count)]
     targets = [(above, me), (below, me)] + [(group, p) for p in partners]
     masks = sorted(range(1, member_count), key=lambda mask: (mask == 1, (mask >> 1).bit_count(), mask & 1))
-    sending = [1 + mask for mask in masks] + [0, 1]
+    sending = [0, 1] + [1 + mask for mask in masks]
 
     labs, lab_sends, lab_recvs = (lab_low, lab_high), (send_low, send_high), (recv_low, recv_high)
     split = lab_low.shape[1]

time: 79.2 us -> 79.2 us (level)
  no operation moved by 1% of the time
where the time goes in v4:
time: 79.2 us; the launch traced here: 78.6 us
  Pallas kernels  76.7 us (97%)
  other arithmetic  1.84 us (2%)
    pallas_call x1, Pallas kernels, direct_body(): pl.pallas_call(functools.partial(direct_kernel, member_count, group_count...  76.7 us
    mul x1, other arithmetic, direct_body(): return sharp.T * classes  1.84 us

profile of v4, /device:TPU:0, one launch (start us, length us, event | category | flops | bytes accessed | tf_op | source)
XLA Modules:
  0.0 78.6 jit_solution(11065037712296583873)
XLA Ops:
  0.0 76.7 %shard_map.64 = f32[1000,768]{1,0:T(8,128)S(1)} custom-call(s32[4,8]{1,0:T(4,128)} %bitcast.17, s32[4,8]{1,0:T(4,128)} %bitcast.18, s32[2,4]{1,0:T(2,128)} %bitcast.19, bf16[6,128,1024]{2,1,0:T(8,128)(2,1)} %bitcast.15, f32[1000,768]{1,0:T(8,128)} %bitcast.14, s32[4,768]{1,0:T(4,128)} %bitcast.16), custom_call_target="tpu_custom_call" | custom-call | tf_op jit(solution)/shard_map/pallas_call | solution.py:404
  76.7 1.8 %multiply_bitcast_fusion = f32[768,1000]{0,1:T(8,128)} fusion(f32[1000,768]{1,0:T(8,128)S(1)} %shard_map.64), kind=kLoop, calls=%fused_computation | loop fusion | flops 768000 | bytes 6144000 | tf_op jit(solution)/shard_map/mul | solution.py:439
